TPU v7x, 32 devices: a whole 2x2x4 slice. The times are simulated.
32 devices in a mesh: tm: 8 (over z, core), space: 2 (over x), samples: 2 (over y).
Axes of the slice: x: 2, y: 2, z: 4, core: 2. Of those that a mesh axis runs over, the one named last changes fastest.
Arguments:
- fields: bfloat16 [2, 16, 16, 128, 256], P('samples', 'tm', 'space'), may hold values from -6 to 6
- out_grad: bfloat16 [2, 16, 16, 128, 256], P('samples', 'tm', 'space'), may hold values from -6 to 6
- spatial_weight: bfloat16 [3, 3, 256, 256], replicated, may hold values from -0.125 to 0.125
- temporal_weight: bfloat16 [5, 256, 256], replicated, may hold values from -0.15625 to 0.15625
Outputs:
- block_out: bfloat16 [2, 16, 16, 128, 256], P('samples', 'tm', 'space')
- fields_grad: bfloat16 [2, 16, 16, 128, 256], P('samples', 'tm', 'space')
- spatial_grad: float32 [3, 3, 256, 256], replicated
- temporal_grad: float32 [5, 256, 256], replicated
All inputs are finite; a program needn't handle non-finite values.
Results may differ from a plain program's by a relative error of at most 0.012.
Values may be sent and summed in bfloat16 or wider, within the bound.
A program may use at most 128 MiB of HBM per device.

v0:
```python
import jax
import jax.numpy as jnp
from jax import lax
from jax.sharding import PartitionSpec as P


def padded_2(shard, sides, width, wrap):
    for axis, dim in sides:
        peers, length = (lax.axis_size(axis), shard.shape[dim])
        up = [(i, (i + 1) % peers) for i in range(peers if wrap else peers - 1)]
        down = [(j, i) for i, j in up]
        last = lax.slice_in_dim(shard, length - width, length, axis=dim)
        first = lax.slice_in_dim(shard, 0, width, axis=dim)
        before = lax.ppermute(last, axis, up)
        after = lax.ppermute(first, axis, down)
        shard = jnp.concatenate([before, shard, after], axis=dim)
    return shard


def gelu_tanh(value):
    return jax.nn.gelu(value, approximate=True)


def pad_cells(field):
    return jnp.pad(field, ((0, 0), (0, 0), (0, 0), (1, 1), (0, 0)))


def spatial_apply(padded, weight, offset, transpose):
    shape = padded.shape
    rows = shape[2] - 2
    cells = shape[3] - 2
    chans = shape[4]
    total = jnp.zeros((shape[0], shape[1], rows, cells, chans), jnp.float32)
    for i in range(3):
        for j in range(3):
            si = offset - i if transpose else i
            sj = offset - j if transpose else j
            piece = padded[:, :, si : si + rows, sj : sj + cells, :].reshape(-1, chans)
            tap = weight[i, j].T if transpose else weight[i, j]
            total = total + jnp.dot(piece, tap, preferred_element_type=jnp.float32).reshape(
                total.shape
            )
    return total


def temporal_apply(act_pad, grad_pad, weight, nframes):
    chans = act_pad.shape[4]
    shape = (act_pad.shape[0], nframes) + act_pad.shape[2:]
    middle = grad_pad[:, 2 : 2 + nframes].reshape(-1, chans)
    block = jnp.zeros(shape, jnp.float32)
    act_grad = jnp.zeros(shape, jnp.float32)
    sums = []
    for k in range(5):
        shifted = act_pad[:, k : k + nframes].reshape(-1, chans)
        block = block + jnp.dot(shifted, weight[k], preferred_element_type=jnp.float32).reshape(
            shape
        )
        sums.append(jnp.dot(shifted.T, middle, preferred_element_type=jnp.float32))
        back = grad_pad[:, 4 - k : 4 - k + nframes].reshape(-1, chans)
        act_grad = act_grad + jnp.dot(
            back, weight[k].T, preferred_element_type=jnp.float32
        ).reshape(shape)
    return (block.astype(jnp.bfloat16), act_grad.astype(jnp.bfloat16), jnp.stack(sums))


def shards(fields, out_grad, spatial_weight, temporal_weight):
    chans = fields.shape[4]
    padded = pad_cells(padded_2(fields, (("space", 2),), 1, True))
    hidden = spatial_apply(padded, spatial_weight, 0, False)
    act = gelu_tanh(hidden).astype(jnp.bfloat16)
    stacked = jnp.stack([act, out_grad])
    margined = padded_2(stacked, (("tm", 2),), 2, False)
    block_out, act_grad, temporal_sum = temporal_apply(
        margined[0], margined[1], temporal_weight, act.shape[1]
    )
    _, pullback = jax.vjp(gelu_tanh, hidden)
    hidden_grad = pullback(act_grad.astype(jnp.float32))[0].astype(jnp.bfloat16)
    rows_hg = hidden_grad.reshape(-1, chans)
    height = fields.shape[2]
    wide = fields.shape[3]
    spatial_list = []
    for i in range(3):
        for j in range(3):
            piece = padded[:, :, i : i + height, j : j + wide, :].reshape(-1, chans)
            spatial_list.append(jnp.dot(piece.T, rows_hg, preferred_element_type=jnp.float32))
    spatial_sum = jnp.stack(spatial_list).reshape(3, 3, chans, chans)
    grad_padded = pad_cells(padded_2(hidden_grad, (("space", 2),), 1, True))
    fields_grad = spatial_apply(grad_padded, spatial_weight, 2, True).astype(jnp.bfloat16)
    all_rows = (
        fields.shape[0]
        * fields.shape[1]
        * height
        * wide
        * lax.axis_size("tm")
        * lax.axis_size("space")
        * lax.axis_size("samples")
    )
    factor = all_rows ** (-0.5)
    spatial_total, temporal_total = lax.psum(
        (spatial_sum, temporal_sum), ("tm", "space", "samples")
    )
    return (block_out, fields_grad, spatial_total * factor, temporal_total * factor)


def solution(mesh):
    return jax.shard_map(
        shards,
        mesh=mesh,
        in_specs=(
            P("samples", "tm", "space", None, None),
            P("samples", "tm", "space", None, None),
            P(),
            P(),
        ),
        out_specs=(
            P("samples", "tm", "space", None, None),
            P("samples", "tm", "space", None, None),
            P(),
            P(),
        ),
        check_vma=False,
    )
```

profile of v0, /device:TPU:0, one launch (start us, length us, event | category | flops | bytes accessed | tf_op | source)
XLA Modules:
  0.0 237.6 jit_solution(12061235643872717782)
XLA Ops:
  7.2 1.0 fusion.130
  8.2 3.0 %collective-permute-start = (bf16[1,2,1,128,256]{4,3,2,1,0:T(8,128)(2,1)S(1)}, bf16[1,2,1,128,256]{4,3,2,1,0:T(8,128)(2,1)S(1)}, u32[]{:S(2)}, u32[]{:S(2)}) collective-permute-start(bf16[1,2,1,128,256]{4,3,2,1,0:T(8,128)(2,1)S(1)} %get-tuple-element.10), channel_id=1, source_target_pairs={{0,2},{2,0},{1,3},{3,1},{4,6},{6,4},{5,7},{7,5},{8,10},{10,8},{9,1... | collective-permute-start | bytes 393224 | tf_op jit(solution)/shard_map/ppermute | solution.py:14
  11.3 1.7 fusion.47
  13.1 2.5 %collective-permute-done = bf16[1,2,1,128,256]{4,3,2,1,0:T(8,128)(2,1)S(1)} collective-permute-done((bf16[1,2,1,128,256]{4,3,2,1,0:T(8,128)(2,1)S(1)}, bf16[1,2,1,128,256]{4,3,2,1,0:T(8,128)(2,1)S(1)}, u32[]{:S(2)}, u32[]{:S(2)}) %collective-permute-start) | collective-permute-done | bytes 131104 | tf_op jit(solution)/shard_map/ppermute | solution.py:14
  15.6 2.0 collective-permute-done.1
  17.5 0.7 select_maximum_fusion.2
  21.4 1.4 add_add_fusion
  22.7 0.7 fusion.49
  23.4 0.6 copy-done.3
  24.1 1.3 collective-permute-start.3
  25.4 3.3 %collective-permute-start.2 = (bf16[2,1,2,8,128,256]{5,4,3,2,1,0:T(8,128)(2,1)S(1)}, bf16[2,1,2,8,128,256]{5,4,3,2,1,0:T(8,128)(2,1)S(1)}, u32[]{:S(2)}, u32[]{:S(2)}) collective-permute-start(bf16[2,1,2,8,128,256]{5,4,3,2,1,0:T(8,128)(2,1)S(1)} %pad_maximum_fusion.1), channel_id=1, source_target_pairs={{0,4},{4,8},{8,12},{12,16},{16,20},{20,24},{24,28},{1,5},{5,9},{9,... | collective-permute-start | bytes 6291464 | tf_op jit(solution)/shard_map/ppermute | solution.py:14
  28.8 1.4 collective-permute-done.3
  30.2 2.1 collective-permute-done.2
  32.3 3.9 %pad_maximum_fusion = bf16[2,1,6,8,128,256]{5,4,3,2,1,0:T(8,128)(2,1)S(1)} fusion(bf16[2,1,2,8,128,256]{5,4,3,2,1,0:T(8,128)(2,1)S(1)} %collective-permute-done.3, bf16[1,1,2,8,128,256]{5,4,3,2,1,0:T(8,128)(2,1)S(1)} %bitcast.367, bf16[1,1,2,8,128,256]{5,4,3,2,1,0:T(8,128)(2,1)S(1)} %fusion.49, bf16[2,1,2,8,128,256]{5,4,3,2,1,0:T(8,128)(2,1)S(1)} %collective-permute-done.2), kind=kLoop, calls=%fused_computation | loop fusion | flops 9437184 | bytes 12582912 | tf_op jit(solution)/shard_map/concatenate | solution.py:16
  36.2 0.8 slice_bitcast_fusion
  39.1 1.2 fusion.18
  40.3 1.8 fusion.59
  42.1 1.8 fusion.58
  43.9 1.8 fusion.57
  45.6 1.8 fusion.56
  47.5 1.2 fusion.17
  48.6 1.2 fusion.16
  49.8 1.2 fusion.15
  51.0 1.2 fusion.14
  52.2 2.2 fusion.3
  54.8 0.7 fusion.129
  55.6 1.7 collective-permute-start.4
  57.6 0.5 fusion.26
  58.1 0.5 fusion.25
  58.6 0.5 fusion.24
  59.1 0.5 fusion.23
  59.6 0.5 fusion.22
  60.1 0.5 fusion.21
  60.6 0.5 fusion.20
  61.2 0.5 fusion.19
  61.7 1.4 copy-done.4
  63.1 1.6 copy-done.2
  64.7 4.9 %fusion.12 = bf16[1,2,8,128,256]{4,3,2,1,0:T(8,128)(2,1)} fusion(f32[2,8,128,256]{3,2,1,0:T(8,128)S(1)} %copy-done.2, f32[2,8,128,256]{3,2,1,0:T(8,128)} %fusion.58, f32[2,8,128,256]{3,2,1,0:T(8,128)} %fusion.56, f32[2,8,128,256]{3,2,1,0:T(8,128)} %fusion.57, bf16[1,6,8,128,256]{4,3,2,1,0:T(8,128)(2,1)} %copy-done, bf16[5,256,256]{2,1,0:T(8,128)(2,1)} %param.7), kind=kOutput, calls=%fused_computation.31 | convolution fusion | flops 271056896 | bytes 10616832 | tf_op jit(solution)/shard_map/dot_general | solution.py:55
  70.0 1.7 select_maximum_fusion
  71.7 0.5 fusion.32
  72.7 0.5 fusion.34
  73.1 1.4 fusion.37
  75.0 0.5 fusion.40
  75.5 0.5 fusion.28
  76.0 3.0 %fusion.13 = bf16[1,2,8,128,256]{4,3,2,1,0:T(8,128)(2,1)} fusion(f32[2,8,128,256]{3,2,1,0:T(8,128)S(1)} %fusion.28, f32[2,8,128,256]{3,2,1,0:T(8,128)S(1)} %fusion.32, f32[2,8,128,256]{3,2,1,0:T(8,128)S(1)} %fusion.33, f32[2,8,128,256]{3,2,1,0:T(8,128)S(1)} %fusion.74, f32[2,8,128,256]{3,2,1,0:T(8,128)S(1)} %fusion.34, f32[2,8,128,256]{3,2,1,0:T(8,128)S(1)} %fusion.35, ...), kind=kOutput, calls=%fused_computation.32 | convolution fusion | flops 273678336 | bytes 19136512 | tf_op jit(solution)/shard_map/dot_general | solution.py:40
  79.0 147.2 %all-reduce.5.cloned.1.call-done = (f32[3,3,256,256]{3,2,1,0:T(8,128)}, f32[5,256,256]{2,1,0:T(8,128)}) async-done(((f32[3,3,256,256]{3,2,1,0:T(8,128)}, f32[5,256,256]{2,1,0:T(8,128)}), (f32[3,3,256,256]{3,2,1,0:T(8,128)}, f32[5,256,256]{2,1,0:T(8,128)})) %all-reduce.5.cloned.1.call-update) | async-done | bytes 3670032 | tf_op jit(solution)/shard_map/psum | solution.py:99
  226.2 3.4 %broadcast_multiply_fusion = f32[3,3,256,256]{3,2,1,0:T(8,128)} fusion(f32[3,3,256,256]{3,2,1,0:T(8,128)} %get-tuple-element.4), kind=kLoop, calls=%fused_computation.33 | loop fusion | flops 589824 | bytes 4718592 | tf_op jit(solution)/shard_map/mul | solution.py:102
  229.5 1.2 broadcast_multiply_fusion.1
  (37 shorter events, 7.7 us)
Async XLA Ops:
  7.2 219.0 %all-reduce.5.cloned.1.call-start = ((), (), s32[]{:S(2)}) async-start(), calls=%async_computation | async-start | bytes 7340032 | tf_op jit(solution)/shard_map/psum | solution.py:99
  8.2 7.4 %collective-permute-start = (bf16[1,2,1,128,256]{4,3,2,1,0:T(8,128)(2,1)S(1)}, bf16[1,2,1,128,256]{4,3,2,1,0:T(8,128)(2,1)S(1)}, u32[]{:S(2)}, u32[]{:S(2)}) collective-permute-start(bf16[1,2,1,128,256]{4,3,2,1,0:T(8,128)(2,1)S(1)} %get-tuple-element.10), channel_id=1, source_target_pairs={{0,2},{2,0},{1,3},{3,1},{4,6},{6,4},{5,7},{7,5},{8,10},{10,8},{9,1... | collective-permute-start | bytes 393224 | tf_op jit(solution)/shard_map/ppermute | solution.py:14
  11.2 6.3 %copy-start.1 = (bf16[1,2,8,128,256]{4,3,2,1,0:T(8,128)(2,1)S(1)}, bf16[1,2,8,128,256]{4,3,2,1,0:T(8,128)(2,1)}, u32[]{:S(2)}) copy-start(bf16[1,2,8,128,256]{4,3,2,1,0:T(8,128)(2,1)} %param.4) | copy-start | bytes 3145732
  11.2 6.3 %collective-permute-start.1 = (bf16[1,2,1,128,256]{4,3,2,1,0:T(8,128)(2,1)S(1)}, bf16[1,2,1,128,256]{4,3,2,1,0:T(8,128)(2,1)S(1)}, u32[]{:S(2)}, u32[]{:S(2)}) collective-permute-start(bf16[1,2,1,128,256]{4,3,2,1,0:T(8,128)(2,1)S(1)} %get-tuple-element.11), channel_id=1, source_target_pairs={{2,0},{0,2},{3,1},{1,3},{6,4},{4,6},{7,5},{5,7},{10,8},{8,10},{11,... | collective-permute-start | bytes 393224 | tf_op jit(solution)/shard_map/ppermute | solution.py:15
  13.1 5.2 %copy-start.6 = (bf16[3,3,256,256]{3,2,1,0:T(8,128)(2,1)S(1)}, bf16[3,3,256,256]{3,2,1,0:T(8,128)(2,1)}, u32[]{:S(2)}) copy-start(bf16[3,3,256,256]{3,2,1,0:T(8,128)(2,1)} %param.6) | copy-start | bytes 3538948
  22.7 1.2 copy-start.3
  24.1 6.1 %collective-permute-start.3 = (bf16[2,1,2,8,128,256]{5,4,3,2,1,0:T(8,128)(2,1)S(1)}, bf16[2,1,2,8,128,256]{5,4,3,2,1,0:T(8,128)(2,1)S(1)}, u32[]{:S(2)}, u32[]{:S(2)}) collective-permute-start(bf16[2,1,2,8,128,256]{5,4,3,2,1,0:T(8,128)(2,1)S(1)} %pad_maximum_fusion.1), channel_id=1, source_target_pairs={{4,0},{8,4},{12,8},{16,12},{20,16},{24,20},{28,24},{5,1},{9,5},{13... | collective-permute-start | bytes 6291464 | tf_op jit(solution)/shard_map/ppermute | solution.py:15
  25.4 6.8 %collective-permute-start.2 = (bf16[2,1,2,8,128,256]{5,4,3,2,1,0:T(8,128)(2,1)S(1)}, bf16[2,1,2,8,128,256]{5,4,3,2,1,0:T(8,128)(2,1)S(1)}, u32[]{:S(2)}, u32[]{:S(2)}) collective-permute-start(bf16[2,1,2,8,128,256]{5,4,3,2,1,0:T(8,128)(2,1)S(1)} %pad_maximum_fusion.1), channel_id=1, source_target_pairs={{0,4},{4,8},{8,12},{12,16},{16,20},{20,24},{24,28},{1,5},{5,9},{9,... | collective-permute-start | bytes 6291464 | tf_op jit(solution)/shard_map/ppermute | solution.py:14
  36.2 1.1 copy-start.5
  37.0 14.0 %copy-start = (bf16[1,6,8,128,256]{4,3,2,1,0:T(8,128)(2,1)}, bf16[1,6,8,128,256]{4,3,2,1,0:T(8,128)(2,1)S(1)}, u32[]{:S(2)}) copy-start(bf16[1,6,8,128,256]{4,3,2,1,0:T(8,128)(2,1)S(1)} %get-tuple-element.7) | copy-start | bytes 9437188
  55.6 14.5 %collective-permute-start.4 = (bf16[1,2,1,128,256]{4,3,2,1,0:T(8,128)(2,1)}, bf16[1,2,1,128,256]{4,3,2,1,0:T(8,128)(2,1)}, u32[]{:S(2)}, u32[]{:S(2)}) collective-permute-start(bf16[1,2,1,128,256]{4,3,2,1,0:T(8,128)(2,1)} %get-tuple-element.8), channel_id=1, source_target_pairs={{0,2},{2,0},{1,3},{3,1},{4,6},{6,4},{5,7},{7,5},{8,10},{10,8},{9,1... | collective-permute-start | bytes 393224 | tf_op jit(solution)/shard_map/ppermute | solution.py:14
  57.3 12.7 %collective-permute-start.5 = (bf16[1,2,1,128,256]{4,3,2,1,0:T(8,128)(2,1)}, bf16[1,2,1,128,256]{4,3,2,1,0:T(8,128)(2,1)}, u32[]{:S(2)}, u32[]{:S(2)}) collective-permute-start(bf16[1,2,1,128,256]{4,3,2,1,0:T(8,128)(2,1)} %get-tuple-element.9), channel_id=1, source_target_pairs={{2,0},{0,2},{3,1},{1,3},{6,4},{4,6},{7,5},{5,7},{10,8},{8,10},{11,... | collective-permute-start | bytes 393224 | tf_op jit(solution)/shard_map/ppermute | solution.py:15
  61.7 1.4 copy-start.4
  63.1 1.6 copy-start.2
  64.7 4.9 %copy-start.7 = (bf16[3,3,256,256]{3,2,1,0:T(8,128)(2,1)S(1)}, bf16[3,3,256,256]{3,2,1,0:T(8,128)(2,1)}, u32[]{:S(2)}) copy-start(bf16[3,3,256,256]{3,2,1,0:T(8,128)(2,1)} %param.6) | copy-start | bytes 3538948
  226.2 3.4 %copy-start.8 = (f32[5,256,256]{2,1,0:T(8,128)S(1)}, f32[5,256,256]{2,1,0:T(8,128)}, u32[]{:S(2)}) copy-start(f32[5,256,256]{2,1,0:T(8,128)} %get-tuple-element.5) | copy-start | bytes 3932164
Sparse Core Ops, SparseCore 0:
  63.2 162.8 all-reduce.4
where the time goes:
time: 238 us
  waiting for transfers between devices  155 us (65%)
  matrix products  40.3 us (17%)
  between operations  14.3 us (6%)
  other arithmetic  11.7 us (5%)
  starting transfers between devices  9.82 us (4%)
  local copies, waits for them, and re-layouts  6.32 us (3%)
    psum x1, waiting for transfers between devices, shards(): lax.psum((spatial_sum, temporal_sum), ('tm', 'space', 'samples'))  147 us
    dot_general x18, matrix products, spatial_apply(): jnp.dot(piece, tap, preferred_element_type=jnp.float32).reshape(total.shape)  13.9 us
    dot_general x5, matrix products, temporal_apply(): jnp.dot(shifted, weight[k], preferred_element_type=jnp.float32)  12 us
    ppermute x3, starting transfers between devices, padded_2(): before = lax.ppermute(last, axis, up)  8.12 us
    concatenate x3, other arithmetic, padded_2(): shard = jnp.concatenate([before, shard, after], axis=dim)  6.28 us
    dot_general x5, matrix products, temporal_apply(): sums.append(jnp.dot(shifted.T, middle, preferred_element_type=jnp.float32))  5.87 us
  transfers between devices with their start and end apart: 7, of which 5 were waited for; matrix products, arithmetic and copies ran while one was open for 8% of the time, Pallas kernels for 0%

commit v1 on v0

--- a/solution.py
+++ b/solution.py
@@ -97,7 +97,7 @@
     )
     factor = all_rows ** (-0.5)
     spatial_total, temporal_total = lax.psum(
-        (spatial_sum, temporal_sum), ("tm", "space", "samples")
+        lax.psum((spatial_sum, temporal_sum), ("space", "samples")), "tm"
     )
     return (block_out, fields_grad, spatial_total * factor, temporal_total * factor)
 

time: 238 us -> 269 us (1.13)
  waiting for transfers between devices: 155 us -> 187 us
    psum x1 -> x2, waiting for transfers between devices: 147 us -> 179 us  [the longest x1 99.5 us: shards(): lax.psum((spatial_sum, temporal_sum), ('space', 'samples'))]
    dot_general x18, matrix products: 13.9 us -> 25.8 us  [spatial_apply(): jnp.dot(piece, tap, preferred_element_type=jnp.float32).reshape(total.shape)]
    dot_general x5, matrix products: 12 us -> 4.7 us  [temporal_apply(): jnp.dot(shifted, weight[k], preferred_element_type=jnp.float32)]
    dot_general x5, matrix products: 5.87 us -> 2.4 us  [temporal_apply(): sums.append(jnp.dot(shifted.T, middle, preferred_element_type=jnp.float32))]
  transfers between devices with their start and end apart: 7 -> 8, of which waited for: 5 -> 6; matrix products, arithmetic and copies ran while one was open for 8% -> 10% of each run, Pallas kernels for 0% -> 0%
where the time goes in v1:
time: 269 us
  waiting for transfers between devices  187 us (70%)
  matrix products  41.2 us (15%)
  between operations  14.4 us (5%)
  other arithmetic  10.8 us (4%)
  starting transfers between devices  10.1 us (4%)
  local copies, waits for them, and re-layouts  5.24 us (2%)
    psum x1, waiting for transfers between devices, shards(): lax.psum((spatial_sum, temporal_sum), ('space', 'samples'))  99.5 us
    psum x1, waiting for transfers between devices, shards(): lax.psum(lax.psum((spatial_sum, temporal_sum), ('space', 'samples')), 'tm')  79.4 us
    dot_general x18, matrix products, spatial_apply(): jnp.dot(piece, tap, preferred_element_type=jnp.float32).reshape(total.shape)  25.8 us
    ppermute x3, starting transfers between devices, padded_2(): before = lax.ppermute(last, axis, up)  8.18 us
    concatenate x3, other arithmetic, padded_2(): shard = jnp.concatenate([before, shard, after], axis=dim)  5.39 us
  transfers between devices with their start and end apart: 8, of which 6 were waited for; matrix products, arithmetic and copies ran while one was open for 10% of the time, Pallas kernels for 0%

profile of v1, /device:TPU:0, one launch (start us, length us, event | category | flops | bytes accessed | tf_op | source)
XLA Modules:
  0.0 268.6 jit_solution(14371255979757460205)
XLA Ops:
  7.2 1.0 fusion.130
  8.2 3.0 %collective-permute-start = (bf16[1,2,1,128,256]{4,3,2,1,0:T(8,128)(2,1)S(1)}, bf16[1,2,1,128,256]{4,3,2,1,0:T(8,128)(2,1)S(1)}, u32[]{:S(2)}, u32[]{:S(2)}) collective-permute-start(bf16[1,2,1,128,256]{4,3,2,1,0:T(8,128)(2,1)S(1)} %get-tuple-element.12), channel_id=1, source_target_pairs={{0,2},{2,0},{1,3},{3,1},{4,6},{6,4},{5,7},{7,5},{8,10},{10,8},{9,1... | collective-permute-start | bytes 393224 | tf_op jit(solution)/shard_map/ppermute | solution.py:14
  11.3 1.7 fusion.47
  13.1 2.5 collective-permute-done
  15.6 2.0 collective-permute-done.1
  17.5 0.7 select_maximum_fusion.2
  21.4 1.3 add_add_fusion
  22.6 0.7 fusion.49
  23.3 0.6 copy-done.5
  24.0 1.3 collective-permute-start.3
  25.3 3.3 %collective-permute-start.2 = (bf16[2,1,2,8,128,256]{5,4,3,2,1,0:T(8,128)(2,1)S(1)}, bf16[2,1,2,8,128,256]{5,4,3,2,1,0:T(8,128)(2,1)S(1)}, u32[]{:S(2)}, u32[]{:S(2)}) collective-permute-start(bf16[2,1,2,8,128,256]{5,4,3,2,1,0:T(8,128)(2,1)S(1)} %pad_maximum_fusion.1), channel_id=1, source_target_pairs={{0,4},{4,8},{8,12},{12,16},{16,20},{20,24},{24,28},{1,5},{5,9},{9,... | collective-permute-start | bytes 6291464 | tf_op jit(solution)/shard_map/ppermute | solution.py:14
  28.7 1.4 collective-permute-done.3
  30.1 2.1 collective-permute-done.2
  32.2 4.0 %pad_maximum_fusion = bf16[2,1,6,8,128,256]{5,4,3,2,1,0:T(8,128)(2,1)S(1)} fusion(bf16[2,1,2,8,128,256]{5,4,3,2,1,0:T(8,128)(2,1)S(1)} %collective-permute-done.3, bf16[1,1,2,8,128,256]{5,4,3,2,1,0:T(8,128)(2,1)S(1)} %bitcast.367, bf16[1,1,2,8,128,256]{5,4,3,2,1,0:T(8,128)(2,1)S(1)} %fusion.49, bf16[2,1,2,8,128,256]{5,4,3,2,1,0:T(8,128)(2,1)S(1)} %collective-permute-done.2), kind=kLoop, calls=%fused_computation | loop fusion | flops 9437184 | bytes 12582912 | tf_op jit(solution)/shard_map/concatenate | solution.py:16
  36.2 0.8 slice_bitcast_fusion
  39.1 0.5 fusion.18
  39.6 0.5 fusion.17
  40.1 0.5 fusion.16
  40.6 0.5 fusion.15
  41.1 0.5 fusion.14
  41.6 2.0 fusion.3
  44.0 0.5 fusion.26
  44.6 0.5 fusion.25
  45.1 0.5 fusion.24
  45.6 0.5 fusion.23
  46.1 0.5 fusion.22
  46.6 0.5 fusion.21
  47.1 0.5 fusion.20
  47.6 0.5 fusion.19
  48.1 1.4 copy-done.6
  49.9 1.8 collective-permute-start.4
  52.0 1.8 fusion.59
  55.4 1.6 fusion.12
  57.0 2.7 %fusion.74 = f32[2,8,128,256]{3,2,1,0:T(8,128)} fusion(bf16[2,8,128,256]{3,2,1,0:T(8,128)(2,1)S(1)} %fusion.3, bf16[3,3,256,256]{3,2,1,0:T(8,128)(2,1)} %param.6), kind=kOutput, calls=%fused_computation.129 | convolution fusion | flops 268435456 | bytes 3276800 | tf_op jit(solution)/shard_map/dot_general | solution.py:40
  59.7 0.7 select_maximum_fusion
  60.4 2.8 %fusion.32 = f32[2,8,128,256]{3,2,1,0:T(8,128)} fusion(bf16[1,2,10,130,256]{4,3,2,1,0:T(8,128)(2,1)S(1)} %select_maximum_fusion, bf16[3,3,256,256]{3,2,1,0:T(8,128)(2,1)} %param.6), kind=kOutput, calls=%fused_computation.68 | convolution fusion | flops 268435456 | bytes 3276800 | tf_op jit(solution)/shard_map/dot_general | solution.py:40
  63.2 2.7 fusion.33
  65.9 2.7 %fusion.34 = f32[2,8,128,256]{3,2,1,0:T(8,128)} fusion(bf16[1,2,10,130,256]{4,3,2,1,0:T(8,128)(2,1)S(1)} %select_maximum_fusion, bf16[3,3,256,256]{3,2,1,0:T(8,128)(2,1)} %param.6), kind=kOutput, calls=%fused_computation.72 | convolution fusion | flops 268435456 | bytes 3276800 | tf_op jit(solution)/shard_map/dot_general | solution.py:40
  68.6 99.5 %all-reduce.9.cloned.1.call-done = (f32[3,3,256,256]{3,2,1,0:T(8,128)}, f32[5,256,256]{2,1,0:T(8,128)}) async-done(((f32[3,3,256,256]{3,2,1,0:T(8,128)}, f32[5,256,256]{2,1,0:T(8,128)}), (f32[3,3,256,256]{3,2,1,0:T(8,128)}, f32[5,256,256]{2,1,0:T(8,128)})) %all-reduce.9.cloned.1.call-update) | async-done | bytes 3670032 | tf_op jit(solution)/shard_map/psum | solution.py:100
  168.1 1.4 fusion.37
  169.5 1.4 fusion.35
  170.9 1.5 fusion.40
  172.4 1.5 fusion.28
  174.3 0.6 copy-done.4
  174.9 3.0 %fusion.13 = bf16[1,2,8,128,256]{4,3,2,1,0:T(8,128)(2,1)} fusion(f32[2,8,128,256]{3,2,1,0:T(8,128)S(1)} %fusion.28, f32[2,8,128,256]{3,2,1,0:T(8,128)S(1)} %copy-done.9, f32[2,8,128,256]{3,2,1,0:T(8,128)S(1)} %copy-done.4, f32[2,8,128,256]{3,2,1,0:T(8,128)S(1)} %copy-done.3, f32[2,8,128,256]{3,2,1,0:T(8,128)S(1)} %copy-done.10, ...), kind=kOutput, calls=%fused_computation.32 | convolution fusion | flops 273678336 | bytes 19136512 | tf_op jit(solution)/shard_map/dot_general | solution.py:40
  177.8 79.4 %all-reduce.7.cloned.1.call-done = (f32[3,3,256,256]{3,2,1,0:T(8,128)}, f32[5,256,256]{2,1,0:T(8,128)}) async-done(((f32[3,3,256,256]{3,2,1,0:T(8,128)}, f32[5,256,256]{2,1,0:T(8,128)}), (f32[3,3,256,256]{3,2,1,0:T(8,128)}, f32[5,256,256]{2,1,0:T(8,128)})) %all-reduce.7.cloned.1.call-update) | async-done | bytes 3670032 | tf_op jit(solution)/shard_map/psum | solution.py:99
  257.2 3.4 %broadcast_multiply_fusion = f32[3,3,256,256]{3,2,1,0:T(8,128)} fusion(f32[3,3,256,256]{3,2,1,0:T(8,128)} %get-tuple-element.4), kind=kLoop, calls=%fused_computation.33 | loop fusion | flops 589824 | bytes 4718592 | tf_op jit(solution)/shard_map/mul | solution.py:102
  260.6 1.2 broadcast_multiply_fusion.1
  (50 shorter events, 8.5 us)
Async XLA Ops:
  7.2 160.9 %all-reduce.9.cloned.1.call-start = ((), (), s32[]{:S(2)}) async-start(), calls=%async_computation.1 | async-start | bytes 7340032 | tf_op jit(solution)/shard_map/psum | solution.py:100
  8.2 7.4 %collective-permute-start = (bf16[1,2,1,128,256]{4,3,2,1,0:T(8,128)(2,1)S(1)}, bf16[1,2,1,128,256]{4,3,2,1,0:T(8,128)(2,1)S(1)}, u32[]{:S(2)}, u32[]{:S(2)}) collective-permute-start(bf16[1,2,1,128,256]{4,3,2,1,0:T(8,128)(2,1)S(1)} %get-tuple-element.12), channel_id=1, source_target_pairs={{0,2},{2,0},{1,3},{3,1},{4,6},{6,4},{5,7},{7,5},{8,10},{10,8},{9,1... | collective-permute-start | bytes 393224 | tf_op jit(solution)/shard_map/ppermute | solution.py:14
  11.2 6.3 %copy-start.2 = (bf16[1,2,8,128,256]{4,3,2,1,0:T(8,128)(2,1)S(1)}, bf16[1,2,8,128,256]{4,3,2,1,0:T(8,128)(2,1)}, u32[]{:S(2)}) copy-start(bf16[1,2,8,128,256]{4,3,2,1,0:T(8,128)(2,1)} %param.4) | copy-start | bytes 3145732
  11.2 6.3 %collective-permute-start.1 = (bf16[1,2,1,128,256]{4,3,2,1,0:T(8,128)(2,1)S(1)}, bf16[1,2,1,128,256]{4,3,2,1,0:T(8,128)(2,1)S(1)}, u32[]{:S(2)}, u32[]{:S(2)}) collective-permute-start(bf16[1,2,1,128,256]{4,3,2,1,0:T(8,128)(2,1)S(1)} %get-tuple-element.13), channel_id=1, source_target_pairs={{2,0},{0,2},{3,1},{1,3},{6,4},{4,6},{7,5},{5,7},{10,8},{8,10},{11,... | collective-permute-start | bytes 393224 | tf_op jit(solution)/shard_map/ppermute | solution.py:15
  13.1 5.2 %copy-start.11 = (bf16[3,3,256,256]{3,2,1,0:T(8,128)(2,1)S(1)}, bf16[3,3,256,256]{3,2,1,0:T(8,128)(2,1)}, u32[]{:S(2)}) copy-start(bf16[3,3,256,256]{3,2,1,0:T(8,128)(2,1)} %param.6) | copy-start | bytes 3538948
  22.6 1.2 copy-start.5
  24.0 6.1 %collective-permute-start.3 = (bf16[2,1,2,8,128,256]{5,4,3,2,1,0:T(8,128)(2,1)S(1)}, bf16[2,1,2,8,128,256]{5,4,3,2,1,0:T(8,128)(2,1)S(1)}, u32[]{:S(2)}, u32[]{:S(2)}) collective-permute-start(bf16[2,1,2,8,128,256]{5,4,3,2,1,0:T(8,128)(2,1)S(1)} %pad_maximum_fusion.1), channel_id=1, source_target_pairs={{4,0},{8,4},{12,8},{16,12},{20,16},{24,20},{28,24},{5,1},{9,5},{13... | collective-permute-start | bytes 6291464 | tf_op jit(solution)/shard_map/ppermute | solution.py:15
  25.3 6.8 %collective-permute-start.2 = (bf16[2,1,2,8,128,256]{5,4,3,2,1,0:T(8,128)(2,1)S(1)}, bf16[2,1,2,8,128,256]{5,4,3,2,1,0:T(8,128)(2,1)S(1)}, u32[]{:S(2)}, u32[]{:S(2)}) collective-permute-start(bf16[2,1,2,8,128,256]{5,4,3,2,1,0:T(8,128)(2,1)S(1)} %pad_maximum_fusion.1), channel_id=1, source_target_pairs={{0,4},{4,8},{8,12},{12,16},{16,20},{20,24},{24,28},{1,5},{5,9},{9,... | collective-permute-start | bytes 6291464 | tf_op jit(solution)/shard_map/ppermute | solution.py:14
  36.2 1.1 copy-start.7
  37.0 4.1 %copy-start = (bf16[1,6,8,128,256]{4,3,2,1,0:T(8,128)(2,1)}, bf16[1,6,8,128,256]{4,3,2,1,0:T(8,128)(2,1)S(1)}, u32[]{:S(2)}) copy-start(bf16[1,6,8,128,256]{4,3,2,1,0:T(8,128)(2,1)S(1)} %get-tuple-element.9) | copy-start | bytes 9437188
  41.6 2.0 copy-start.12
  48.1 1.4 copy-start.6
  49.6 207.6 %all-reduce.7.cloned.1.call-start = ((), (), s32[]{:S(2)}) async-start(), calls=%async_computation | async-start | bytes 7340032 | tf_op jit(solution)/shard_map/psum | solution.py:99
  49.9 9.8 %collective-permute-start.4 = (bf16[1,2,1,128,256]{4,3,2,1,0:T(8,128)(2,1)S(1)}, bf16[1,2,1,128,256]{4,3,2,1,0:T(8,128)(2,1)S(1)}, u32[]{:S(2)}, u32[]{:S(2)}) collective-permute-start(bf16[1,2,1,128,256]{4,3,2,1,0:T(8,128)(2,1)S(1)} %get-tuple-element.10), channel_id=1, source_target_pairs={{0,2},{2,0},{1,3},{3,1},{4,6},{6,4},{5,7},{7,5},{8,10},{10,8},{9,1... | collective-permute-start | bytes 393224 | tf_op jit(solution)/shard_map/ppermute | solution.py:14
  51.7 2.2 copy-start.1
  51.7 2.4 copy-start.8
  51.7 8.0 %collective-permute-start.5 = (bf16[1,2,1,128,256]{4,3,2,1,0:T(8,128)(2,1)S(1)}, bf16[1,2,1,128,256]{4,3,2,1,0:T(8,128)(2,1)S(1)}, u32[]{:S(2)}, u32[]{:S(2)}) collective-permute-start(bf16[1,2,1,128,256]{4,3,2,1,0:T(8,128)(2,1)S(1)} %get-tuple-element.11), channel_id=1, source_target_pairs={{2,0},{0,2},{3,1},{1,3},{6,4},{4,6},{7,5},{5,7},{10,8},{8,10},{11,... | collective-permute-start | bytes 393224 | tf_op jit(solution)/shard_map/ppermute | solution.py:15
  170.9 3.1 %copy-start.9 = (f32[2,8,128,256]{3,2,1,0:T(8,128)S(1)}, f32[2,8,128,256]{3,2,1,0:T(8,128)}, u32[]{:S(2)}) copy-start(f32[2,8,128,256]{3,2,1,0:T(8,128)} %fusion.32) | copy-start | bytes 6291460
  170.9 3.1 %copy-start.10 = (f32[2,8,128,256]{3,2,1,0:T(8,128)S(1)}, f32[2,8,128,256]{3,2,1,0:T(8,128)}, u32[]{:S(2)}) copy-start(f32[2,8,128,256]{3,2,1,0:T(8,128)} %fusion.34) | copy-start | bytes 6291460
  172.4 1.8 copy-start.3
  172.4 2.4 copy-start.4
  257.2 3.4 %copy-start.13 = (f32[5,256,256]{2,1,0:T(8,128)S(1)}, f32[5,256,256]{2,1,0:T(8,128)}, u32[]{:S(2)}) copy-start(f32[5,256,256]{2,1,0:T(8,128)} %get-tuple-element.5) | copy-start | bytes 3932164
Sparse Core Ops, SparseCore 0:
  49.7 118.3 all-reduce.8
  170.5 86.5 all-reduce.6
